TPU v7x, 32 devices: a whole 2x2x4 slice. The times are simulated.
32 devices in a mesh: dp: 8 (over y, x, core), tensor: 4 (over z).
Axes of the slice: x: 2, y: 2, z: 4, core: 2. Of those that a mesh axis runs over, the one named last changes fastest.
Arguments:
- tokens: bfloat16 [32, 1024, 512], P(('dp', 'tensor')), may hold values from -6 to 6
- timestep: int32 [32], P(('dp', 'tensor')), may hold values from 0 to 999
- segment_ids: int32 [32, 1024], P('dp'), may hold values from 0 to 7, never falling along the last dimension, each value on 1 to 512 neighbouring positions
- span_lengths: int32 [32], P('dp'), may hold values from 512 to 1024
- w_qkv: float32 [3, 512, 512], P(None, 'dp', 'tensor'), may hold values from -0.25 to 0.25
- w_out_t: float32 [512, 512], P('dp', 'tensor'), may hold values from -1.5 to 1.5
- w_up: float32 [512, 2048], P('dp', 'tensor'), may hold values from -0.25 to 0.25
- w_down_t: float32 [512, 2048], P('dp', 'tensor'), may hold values from -0.125 to 0.125
- w_time: float32 [512, 512], replicated, may hold values from -0.25 to 0.25
- b_time: float32 [512], replicated, may hold values from -3 to 3
- ln1_gain: float32 [512], replicated, may hold values from 0.1 to 1.9
- ln1_bias: float32 [512], replicated, may hold values from -3 to 3
- ln2_gain: float32 [512], replicated, may hold values from 0.1 to 1.9
- ln2_bias: float32 [512], replicated, may hold values from -3 to 3
- b_up: float32 [2048], replicated, may hold values from -3 to 3
- b_down: float32 [512], replicated, may hold values from -3 to 3
- cotangent: bfloat16 [32, 1024, 512], P(('dp', 'tensor')), may hold values from -6 to 6
Outputs:
- layer_out: bfloat16 [32, 1024, 512], P(('dp', 'tensor'))
- grad_tokens: float32 [32, 1024, 512], P(('dp', 'tensor'))
- grad_w_qkv: float32 [3, 512, 512], P(None, 'dp', 'tensor')
- grad_w_out_t: float32 [512, 512], P('dp', 'tensor')
- grad_w_up: float32 [512, 2048], P('dp', 'tensor')
- grad_w_down_t: float32 [512, 2048], P('dp', 'tensor')
- grad_w_time: float32 [512, 512], replicated
- grad_b_time: float32 [512], replicated
- grad_ln1_gain: float32 [512], replicated
- grad_ln1_bias: float32 [512], replicated
- grad_ln2_gain: float32 [512], replicated
- grad_ln2_bias: float32 [512], replicated
- grad_b_up: float32 [2048], replicated
- grad_b_down: float32 [512], replicated
Inputs may be any that keep to these rules, and one draw needn't show every extreme that they name: `segment_ids`: never falls along a row; each document has 1 to 512 positions and one has exactly that many.
All inputs are finite; a program needn't handle non-finite values.
Results may differ from a plain program's by a relative error of at most 0.013.
Values may be sent and summed in bfloat16 or wider, within the bound.
A program may use at most 192 MiB of HBM per device.

v0:
```python
import math
import jax
import jax.numpy as jnp
from jax import lax
from jax.sharding import PartitionSpec as P

HS = 64
FF = 2048
highest = lax.Precision.HIGHEST
epsilon = 1e-05
masked_score = -1e30


def split_up(value, dim, count):
    before, after = (value.shape[:dim], value.shape[dim + 1 :])
    return jnp.moveaxis(value.reshape(*before, count, -1, *after), dim, 0)


def sent_and_summed(value, axis, dim):
    count = lax.axis_size(axis)
    parts = lax.all_to_all(split_up(value, dim, count), axis, 0, 0, tiled=True)
    return jnp.sum(parts.astype(jnp.float32), axis=0)


def side_by_side(arrays, axis, dim, along):
    ends, at = ([], 0)
    for a in arrays[:-1]:
        at += a.shape[along]
        ends.append(at)
    both = jnp.concatenate(arrays, axis=along)
    return tuple(jnp.split(sent_and_summed(both, axis, dim), ends, axis=along))


def norm_layer(values, gain_vec, shift_vec):
    row_mean = jnp.mean(values, axis=-1, keepdims=True)
    centred = values - row_mean
    variance = jnp.mean(centred * centred, axis=-1, keepdims=True)
    return centred * lax.rsqrt(variance + epsilon) * gain_vec + shift_vec


def time_features(timestep, features):
    half_width = features // 2
    frequency = jnp.exp(-math.log(10000.0) * jnp.arange(half_width, dtype=jnp.float32) / half_width)
    angles = timestep.astype(jnp.float32)[:, None] * frequency[None, :]
    return jnp.concatenate([jnp.sin(angles), jnp.cos(angles)], axis=1)


def allowed_keys(segment, length):
    places = jnp.arange(segment.shape[0], dtype=jnp.int32)
    same_doc = segment[:, None] == segment[None, :]
    is_valid = (places < length)[None, :] | (places[:, None] == places[None, :])
    return same_doc & is_valid


def gelu_tanh(values):
    return jax.nn.gelu(values, approximate=True)


def split_heads(values):
    return values.reshape(values.shape[0], values.shape[1] // HS, HS)


def head_scores(query_heads, key_heads, allowed):
    scores = jnp.einsum(
        "qhe,khe->hqk", query_heads, key_heads, preferred_element_type=jnp.float32
    ) * (1.0 / math.sqrt(HS))
    return jnp.where(allowed[None], scores, masked_score)


def attend_forward(packed):
    query_heads = split_heads(packed[0])
    key_heads = split_heads(packed[1])
    value_heads = split_heads(packed[2])
    scores = head_scores(query_heads, key_heads, allowed_keys(packed[3], packed[4]))
    row_max = jnp.max(scores, axis=-1, keepdims=True)
    raised = jnp.exp(scores - row_max)
    row_total = jnp.sum(raised, axis=-1, keepdims=True)
    probs_low = (raised / row_total).astype(jnp.bfloat16)
    mixed = jnp.einsum("hqk,khe->qhe", probs_low, value_heads, preferred_element_type=jnp.float32)
    return (mixed.reshape(packed[0].shape).astype(jnp.bfloat16), row_max + jnp.log(row_total))


def attend_backward(packed):
    query_heads = split_heads(packed[0])
    key_heads = split_heads(packed[1])
    value_heads = split_heads(packed[2])
    grad_heads = split_heads(packed[3])
    scores = head_scores(query_heads, key_heads, allowed_keys(packed[5], packed[6]))
    attn_probs = jnp.exp(scores - packed[4])
    probs_low = attn_probs.astype(jnp.bfloat16)
    grad_values = jnp.einsum(
        "hqk,qhe->khe", probs_low, grad_heads, preferred_element_type=jnp.float32
    )
    grad_probs = jnp.einsum(
        "qhe,khe->hqk", grad_heads, value_heads, preferred_element_type=jnp.float32
    )
    row_delta = jnp.sum(attn_probs * grad_probs, axis=-1, keepdims=True)
    grad_scores = (attn_probs * (grad_probs - row_delta)).astype(jnp.bfloat16)
    score_scale = 1.0 / math.sqrt(HS)
    grad_queries = (
        jnp.einsum("hqk,khe->qhe", grad_scores, key_heads, preferred_element_type=jnp.float32)
        * score_scale
    )
    grad_keys = (
        jnp.einsum("hqk,qhe->khe", grad_scores, query_heads, preferred_element_type=jnp.float32)
        * score_scale
    )
    shape_rows = packed[0].shape
    return jnp.stack(
        [
            grad_queries.reshape(shape_rows),
            grad_keys.reshape(shape_rows),
            grad_values.reshape(shape_rows),
        ]
    ).astype(jnp.bfloat16)


def shards(
    tokens,
    timestep,
    segment_ids,
    span_lengths,
    w_qkv,
    w_out_t,
    w_up,
    w_down_t,
    w_time,
    b_time,
    ln1_gain,
    ln1_bias,
    ln2_gain,
    ln2_bias,
    b_up,
    b_down,
    cotangent,
):
    tensor_place = lax.axis_index("tensor")
    qkv_copy, out_copy, up_copy, down_copy = (
        lax.all_gather(w_qkv.astype(jnp.bfloat16), "dp", axis=1, tiled=True),
        lax.all_gather(w_out_t.astype(jnp.bfloat16), "dp", axis=0, tiled=True),
        lax.all_gather(w_up.astype(jnp.bfloat16), "dp", axis=0, tiled=True),
        lax.all_gather(w_down_t.astype(jnp.bfloat16), "dp", axis=0, tiled=True),
    )
    bias_up_cols = lax.dynamic_slice_in_dim(
        b_up, tensor_place * up_copy.shape[1], up_copy.shape[1], 0
    )
    ff_cols = up_copy.shape[1]
    time_emb = time_features(timestep, tokens.shape[2])
    time_proj = jnp.dot(time_emb, w_time, precision=highest) + b_time
    start = tokens.astype(jnp.float32) + time_proj[:, None, :]
    normed_one = norm_layer(start, ln1_gain, ln1_bias).astype(jnp.bfloat16)
    normed_all = lax.all_gather(normed_one, "tensor", axis=0, tiled=True)
    qkv_act = jnp.einsum(
        "nsd,cde->cnse", normed_all, qkv_copy, preferred_element_type=jnp.float32
    ).astype(jnp.bfloat16)
    mixed, log_total = lax.map(
        attend_forward, (qkv_act[0], qkv_act[1], qkv_act[2], segment_ids, span_lengths)
    )
    part_rows = mixed
    attn_out = lax.psum_scatter(
        jnp.einsum("nse,de->nsd", part_rows, out_copy, preferred_element_type=jnp.float32),
        "tensor",
        scatter_dimension=0,
        tiled=True,
    )
    middle = start + attn_out
    normed_two = norm_layer(middle, ln2_gain, ln2_bias).astype(jnp.bfloat16)
    second_all = lax.all_gather(normed_two, "tensor", axis=0, tiled=True)
    upper = (
        jnp.einsum("nsd,df->nsf", second_all, up_copy, preferred_element_type=jnp.float32)
        + bias_up_cols
    )
    activated = gelu_tanh(upper).astype(jnp.bfloat16)
    part_rows = activated
    ffn_out = lax.psum_scatter(
        jnp.einsum("nsf,df->nsd", part_rows, down_copy, preferred_element_type=jnp.float32).astype(
            jnp.bfloat16
        ),
        "tensor",
        scatter_dimension=0,
        tiled=True,
    ).astype(jnp.float32)
    layer_out = (middle + ffn_out + b_down).astype(jnp.bfloat16)
    grad_b_down = jnp.sum(cotangent.astype(jnp.float32), axis=(0, 1))
    grad_out_all = lax.all_gather(cotangent, "tensor", axis=0, tiled=True)
    grad_down = jnp.einsum(
        "nsd,nsf->df", grad_out_all, activated, preferred_element_type=jnp.float32
    )
    grad_act = jnp.einsum(
        "nsd,df->nsf", grad_out_all, down_copy, preferred_element_type=jnp.float32
    )
    gelu_value, gelu_pull = jax.vjp(gelu_tanh, upper)
    grad_upper = gelu_pull(grad_act)[0].astype(jnp.bfloat16)
    grad_bias_cols = jnp.sum(grad_upper.astype(jnp.float32), axis=(0, 1))
    grad_up = jnp.einsum("nsd,nsf->df", second_all, grad_upper, preferred_element_type=jnp.float32)
    part_rows = grad_upper
    grad_normed_two = lax.psum_scatter(
        jnp.einsum("nsf,df->nsd", part_rows, up_copy, preferred_element_type=jnp.float32).astype(
            jnp.bfloat16
        ),
        "tensor",
        scatter_dimension=0,
        tiled=True,
    ).astype(jnp.float32)
    norm_two_value, norm_two_pull = jax.vjp(norm_layer, middle, ln2_gain, ln2_bias)
    grad_middle_norm, grad_gain_two, grad_bias_two = norm_two_pull(grad_normed_two)
    grad_middle = cotangent.astype(jnp.float32) + grad_middle_norm
    grad_attn = grad_middle.astype(jnp.bfloat16)
    grad_attn_all = lax.all_gather(grad_attn, "tensor", axis=0, tiled=True)
    grad_out_w = jnp.einsum("nsd,nse->de", grad_attn_all, mixed, preferred_element_type=jnp.float32)
    grad_mixed = jnp.einsum(
        "nsd,de->nse", grad_attn_all, out_copy, preferred_element_type=jnp.float32
    ).astype(jnp.bfloat16)
    grad_qkv_act = lax.map(
        attend_backward,
        (qkv_act[0], qkv_act[1], qkv_act[2], grad_mixed, log_total, segment_ids, span_lengths),
    )
    grad_qkv_w = jnp.einsum(
        "nsd,ncse->cde", normed_all, grad_qkv_act, preferred_element_type=jnp.float32
    )
    part_rows = grad_qkv_act
    grad_normed_one = lax.psum_scatter(
        jnp.einsum("ncse,cde->nsd", part_rows, qkv_copy, preferred_element_type=jnp.float32).astype(
            jnp.bfloat16
        ),
        "tensor",
        scatter_dimension=0,
        tiled=True,
    ).astype(jnp.float32)
    norm_one_value, norm_one_pull = jax.vjp(norm_layer, start, ln1_gain, ln1_bias)
    grad_start_norm, grad_gain_one, grad_bias_one = norm_one_pull(grad_normed_one)
    grad_tokens = grad_middle + grad_start_norm
    grad_time_rows = jnp.sum(grad_tokens, axis=1)
    grad_time_w = jnp.dot(time_emb.T, grad_time_rows, precision=highest)
    grad_time_bias = jnp.sum(grad_time_rows, axis=0)
    grad_bias_up = lax.dynamic_update_slice_in_dim(
        jnp.zeros((FF,), jnp.float32), grad_bias_cols, tensor_place * ff_cols, 0
    )
    shard_qkv, shard_out, shard_up, shard_down = (
        sent_and_summed(grad_qkv_w.astype(jnp.bfloat16), "dp", 1),
        *side_by_side(
            (
                grad_out_w.astype(jnp.bfloat16),
                grad_up.astype(jnp.bfloat16),
                grad_down.astype(jnp.bfloat16),
            ),
            "dp",
            0,
            1,
        ),
    )
    summed = lax.psum(
        (
            grad_time_w,
            grad_time_bias,
            grad_gain_one,
            grad_bias_one,
            grad_gain_two,
            grad_bias_two,
            grad_bias_up,
            grad_b_down,
        ),
        ("dp", "tensor"),
    )
    return (
        layer_out,
        grad_tokens,
        shard_qkv,
        shard_out,
        shard_up,
        shard_down,
        summed[0],
        summed[1],
        summed[2],
        summed[3],
        summed[4],
        summed[5],
        summed[6],
        summed[7],
    )


def solution(mesh):
    return jax.shard_map(
        shards,
        mesh=mesh,
        in_specs=(
            P(("dp", "tensor"), None, None),
            P(("dp", "tensor")),
            P("dp", None),
            P("dp"),
            P(None, "dp", "tensor"),
            P("dp", "tensor"),
            P("dp", "tensor"),
            P("dp", "tensor"),
            P(),
            P(),
            P(),
            P(),
            P(),
            P(),
            P(),
            P(),
            P(("dp", "tensor"), None, None),
        ),
        out_specs=(
            P(("dp", "tensor"), None, None),
            P(("dp", "tensor"), None, None),
            P(None, "dp", "tensor"),
            P("dp", "tensor"),
            P("dp", "tensor"),
            P("dp", "tensor"),
            P(),
            P(),
            P(),
            P(),
            P(),
            P(),
            P(),
            P(),
        ),
        check_vma=False,
    )
```

profile of v0, /device:TPU:0, one launch (start us, length us, event | category | flops | bytes accessed | tf_op | source)
XLA Modules:
  0.0 1040.7 jit_solution(14734776910179383602)
XLA Ops:
  13.0 2.7 add_convert_fusion.2
  15.9 10.7 %all_gather.26 = bf16[512,128]{1,0:T(8,128)(2,1)S(1)} all-gather(bf16[64,128]{1,0:T(8,128)(2,1)S(1)} %convert_element_type.133), channel_id=1, replica_groups=mesh['dp'=8,'tensor'=4] {'dp'}, dimensions={0}, use_global_device_ids=true | all-gather | bytes 147456 | tf_op jit(solution)/shard_map/all_gather | solution.py:140
  26.6 9.7 all_gather.25
  36.3 63.1 %all-gather.5.cloned.1.call-done = bf16[4,1024,512]{2,1,0:T(8,128)(2,1)} async-done(((bf16[1,1024,512]{2,1,0:T(8,128)(2,1)}), bf16[4,1024,512]{2,1,0:T(8,128)(2,1)}) %all-gather.5.cloned.1.call-update) | async-done | bytes 4194320 | tf_op jit(solution)/shard_map/all_gather | solution.py:152
  99.4 4.5 convert_bitcast_fusion
  109.8 42.4 %while.22 = (s32[]{:T(128)}, bf16[4,1024,128]{1,2,0:T(8,128)(2,1)S(1)}, f32[4,2,1024,1]{2,1,3,0:T(2,128)S(1)}, bf16[4,1024,128]{1,2,0:T(8,128)(2,1)S(1)}, s32[4,...) while((s32[]{:T(128)}, ...), condition=%wide.region_5.6_spmd, body=%wide.region_2.5_spmd.sunk | while | flops 566361088 | bytes 32585864 | solution.py:156
  117.5 2.8 fusion.136
  128.1 2.8 fusion.136
  138.7 2.8 fusion.136
  149.3 2.8 fusion.136
  152.2 4.5 fusion.69
  156.9 143.1 %reduce-scatter.5.cloned.1.call-done = f32[1,1024,512]{2,1,0:T(8,128)} async-done(((f32[4,1024,512]{2,1,0:T(8,128)}), f32[1,1024,512]{2,1,0:T(8,128)}) %reduce-scatter.5.cloned.1.call-update) | async-done | bytes 2097168 | tf_op jit(solution)/shard_map/reduce_scatter | solution.py:160
  305.2 10.2 all_gather.29
  315.4 9.8 all_gather.28
  325.2 60.2 %all-gather.7.cloned.1.call-done = bf16[4,1024,512]{2,1,0:T(8,128)(2,1)} async-done(((bf16[1,1024,512]{2,1,0:T(8,128)(2,1)}), bf16[4,1024,512]{2,1,0:T(8,128)(2,1)}) %all-gather.7.cloned.1.call-update) | async-done | bytes 4194320 | tf_op jit(solution)/shard_map/all_gather | solution.py:168
  385.5 8.0 fusion.64
  393.4 72.8 %all-gather.9.cloned.1.call-done = bf16[4,1024,512]{2,1,0:T(8,128)(2,1)} async-done(((bf16[1,1024,512]{2,1,0:T(8,128)(2,1)}), bf16[4,1024,512]{2,1,0:T(8,128)(2,1)}) %all-gather.9.cloned.1.call-update) | async-done | bytes 4194320 | tf_op jit(solution)/shard_map/all_gather | solution.py:185
  466.2 10.3 convert_reduce_fusion
  478.5 4.5 convolution_convert_fusion
  483.1 8.8 convolution_convert_fusion.1
  491.9 66.5 %reduce-scatter.9.cloned.1.call-done = bf16[1,1024,512]{2,1,0:T(8,128)(2,1)} async-done(((bf16[4,1024,512]{2,1,0:T(8,128)(2,1)}), bf16[1,1024,512]{2,1,0:T(8,128)(2,1)}) %reduce-scatter.9.cloned.1.call-update) | async-done | bytes 1048592 | tf_op jit(solution)/shard_map/reduce_scatter | solution.py:197
  558.5 2.7 fusion.40
  561.2 76.8 %reduce-scatter.7.cloned.1.call-done = bf16[1,1024,512]{2,1,0:T(8,128)(2,1)} async-done(((bf16[4,1024,512]{2,1,0:T(8,128)(2,1)}), bf16[1,1024,512]{2,1,0:T(8,128)(2,1)}) %reduce-scatter.7.cloned.1.call-update) | async-done | bytes 1048592 | tf_op jit(solution)/shard_map/reduce_scatter | solution.py:175
  638.0 3.2 fusion.78
  644.2 81.2 %all-gather.11.cloned.1.call-done = bf16[4,1024,512]{2,1,0:T(8,128)(2,1)} async-done(((bf16[1,1024,512]{2,1,0:T(8,128)(2,1)}), bf16[4,1024,512]{2,1,0:T(8,128)(2,1)}) %all-gather.11.cloned.1.call-update) | async-done | bytes 4194320 | tf_op jit(solution)/shard_map/all_gather | solution.py:209
  725.3 3.4 convolution_convert_fusion.2
  728.8 72.6 %while.23 = (s32[]{:T(128)}, bf16[4,3,1024,128]{2,3,1,0:T(8,128)(2,1)}, bf16[4,1024,128]{1,2,0:T(8,128)(2,1)}, s32[4,1024]{1,0:T(4,128)S(1)}, s32[4]{0:T(128)S(1...) while((s32[]{:T(128)}, ...), condition=%wide.region_15.16_spmd, body=%wide.region_13.15_spmd.sunk | while | flops 1380842496 | bytes 73996440 | solution.py:214
  737.6 3.4 multiply_reduce_fusion.4
  741.1 2.7 multiply_convert_fusion.5
  755.8 3.4 multiply_reduce_fusion.4
  759.2 2.7 multiply_convert_fusion.5
  773.9 3.4 multiply_reduce_fusion.4
  777.4 2.7 multiply_convert_fusion.5
  792.1 3.4 multiply_reduce_fusion.4
  795.5 2.7 multiply_convert_fusion.5
  801.4 6.3 bitcast_convert_fusion
  809.3 6.5 fusion.47
  815.9 7.1 fusion.55
  825.3 5.1 fusion.57
  831.4 3.8 all-to-all-start
  835.2 47.9 %reduce-scatter.11.cloned.1.call-done = bf16[1,1024,512]{2,1,0:T(8,128)(2,1)} async-done(((bf16[4,1024,512]{2,1,0:T(8,128)(2,1)}), bf16[1,1024,512]{2,1,0:T(8,128)(2,1)}) %reduce-scatter.11.cloned.1.call-update) | async-done | bytes 1048592 | tf_op jit(solution)/shard_map/reduce_scatter | solution.py:222
  883.2 2.7 convert_reduce_fusion.1
  885.9 3.1 fusion.41
  889.0 4.2 all-to-all-start.1
  893.3 4.4 fusion.77
  900.1 10.1 all-to-all-done.1
  913.0 41.1 %all-reduce = (f32[512]{0:T(512)}, f32[512]{0:T(512)}, f32[512]{0:T(512)}, f32[512]{0:T(512)}, f32[512]{0:T(512)}, /*index=5*/f32[2048]{0:T(1024)}, f32[512]{0:T(512)}) all-reduce(f32[512]{0:T(512)} %copy-done.32, f32[512]{0:T(512)S(1)} %copy-done.38, f32[512]{0:T(512)S(1)} %copy-done.37, ...), channel_id=1, replica_groups=mesh['dp'=8,'tensor'=4] {'dp','tensor'}, use_global_device_ids=true, to_apply=%region_23.24 | all-reduce | flops 5120 | bytes 40960 | tf_op jit(solution)/shard_map/psum | solution.py:252
  954.1 77.5 %all-reduce.3.cloned.1.call-done = f32[512,512]{1,0:T(8,128)} async-done(((f32[512,512]{1,0:T(8,128)}), f32[512,512]{1,0:T(8,128)}) %all-reduce.3.cloned.1.call-update) | async-done | bytes 1048592 | tf_op jit(solution)/shard_map/psum | solution.py:252
  (254 shorter events, 112.3 us)
Async XLA Ops:
  7.2 8.6 copy-start.27
  7.2 8.6 copy-start.21
  7.2 92.1 %all-gather.5.cloned.1.call-start = ((), (), s32[]{:S(2)}) async-start(), calls=%async_computation.6 | async-start | bytes 5242880 | tf_op jit(solution)/shard_map/all_gather | solution.py:152
  9.7 290.2 %copy-start.18 = (f32[512]{0:T(512)}, f32[512]{0:T(512)S(1)}, u32[]{:S(2)}) copy-start(f32[512]{0:T(512)S(1)} %add.138) | copy-start | bytes 6148
  11.3 4.6 copy-start.14
  15.7 284.2 %reduce-scatter.5.cloned.1.call-start = ((), (), s32[]{:S(2)}) async-start(), calls=%async_computation.7 | async-start | bytes 10485760 | tf_op jit(solution)/shard_map/reduce_scatter | solution.py:160
  36.3 67.6 %copy-start.12 = (bf16[3,512,128]{2,1,0:T(8,128)(2,1)}, bf16[3,512,128]{2,1,0:T(8,128)(2,1)S(1)}, u32[]{:S(2)}) copy-start(bf16[3,512,128]{2,1,0:T(8,128)(2,1)S(1)} %all_gather.25) | copy-start | bytes 1179652
  105.4 4.3 copy-start.20
  105.4 4.3 copy-start.46
  152.2 4.6 copy-start.6
  152.2 4.5 copy-start.7
  152.2 4.5 copy-start.10
  156.8 143.2 %copy-start.2 = (bf16[1,1024,512]{2,1,0:T(8,128)(2,1)S(1)}, bf16[1,1024,512]{2,1,0:T(8,128)(2,1)}, u32[]{:S(2)}) copy-start(bf16[1,1024,512]{2,1,0:T(8,128)(2,1)} %param.21) | copy-start | bytes 3145732
  156.8 145.5 %copy-start.31 = (f32[512]{0:T(512)S(1)}, f32[512]{0:T(512)}, u32[]{:S(2)}) copy-start(f32[512]{0:T(512)} %param.33) | copy-start | bytes 6148
  156.8 145.5 %copy-start.43 = (f32[512]{0:T(512)S(1)}, f32[512]{0:T(512)}, u32[]{:S(2)}) copy-start(f32[512]{0:T(512)} %param.34) | copy-start | bytes 6148
  156.8 228.6 %all-gather.7.cloned.1.call-start = ((), (), s32[]{:S(2)}) async-start(), calls=%async_computation.8 | async-start | bytes 5242880 | tf_op jit(solution)/shard_map/all_gather | solution.py:168
  303.7 162.5 %all-gather.9.cloned.1.call-start = ((), (), s32[]{:S(2)}) async-start(), calls=%async_computation.10 | async-start | bytes 5242880 | tf_op jit(solution)/shard_map/all_gather | solution.py:185
  304.3 254.1 %reduce-scatter.9.cloned.1.call-start = ((), (), s32[]{:S(2)}) async-start(), calls=%async_computation.11 | async-start | bytes 5242880 | tf_op jit(solution)/shard_map/reduce_scatter | solution.py:197
  483.0 155.0 %reduce-scatter.7.cloned.1.call-start = ((), (), s32[]{:S(2)}) async-start(), calls=%async_computation.9 | async-start | bytes 5242880 | tf_op jit(solution)/shard_map/reduce_scatter | solution.py:175
  491.8 146.2 %copy-start.44 = (f32[512]{0:T(512)S(1)}, f32[512]{0:T(512)}, u32[]{:S(2)}) copy-start(f32[512]{0:T(512)} %param.36) | copy-start | bytes 6148
  491.9 233.5 %all-gather.11.cloned.1.call-start = ((), (), s32[]{:S(2)}) async-start(), calls=%async_computation.12 | async-start | bytes 5242880 | tf_op jit(solution)/shard_map/all_gather | solution.py:209
  561.2 81.3 %copy-start.8 = (bf16[1,1024,512]{2,1,0:T(8,128)(2,1)S(1)}, bf16[1,1024,512]{2,1,0:T(8,128)(2,1)}, u32[]{:S(2)}) copy-start(bf16[1,1024,512]{2,1,0:T(8,128)(2,1)} %param.37) | copy-start | bytes 3145732
  641.2 87.6 %copy-start.24 = (f32[1024]{0:T(1024)}, f32[1024]{0:T(1024)S(1)}, u32[]{:S(2)}) copy-start(f32[1024]{0:T(1024)S(1)} %negate_multiply_fusion.1) | copy-start | bytes 12292
  643.9 239.2 %reduce-scatter.11.cloned.1.call-start = ((), (), s32[]{:S(2)}) async-start(), calls=%async_computation.13 | async-start | bytes 5242880 | tf_op jit(solution)/shard_map/reduce_scatter | solution.py:222
  728.8 72.6 %copy-start.13 = (bf16[3,512,128]{2,1,0:T(8,128)(2,1)S(1)}, bf16[3,512,128]{2,1,0:T(8,128)(2,1)}, u32[]{:S(2)}) copy-start(bf16[3,512,128]{2,1,0:T(8,128)(2,1)} %copy-done.12) | copy-start | bytes 1179652
  801.4 6.3 copy-start.34
  801.4 6.3 copy-start.36
  809.3 6.5 copy-start.45
  815.8 7.2 copy-start.4
  815.8 7.2 copy-start.11
  825.3 57.9 %copy-start.3 = (bf16[1,1024,512]{2,1,0:T(8,128)(2,1)S(1)}, bf16[1,1024,512]{2,1,0:T(8,128)(2,1)}, u32[]{:S(2)}) copy-start(bf16[1,1024,512]{2,1,0:T(8,128)(2,1)} %param.21) | copy-start | bytes 3145732
  825.3 57.9 %copy-start.15 = (f32[1024]{0:T(1024)S(1)}, f32[1024]{0:T(1024)}, u32[]{:S(2)}) copy-start(f32[1024]{0:T(1024)} %copy-done.14) | copy-start | bytes 12292
  825.3 57.9 %copy-start.19 = (f32[512]{0:T(512)S(1)}, f32[512]{0:T(512)}, u32[]{:S(2)}) copy-start(f32[512]{0:T(512)} %copy-done.18) | copy-start | bytes 6148
  825.3 57.9 %copy-start.30 = (f32[512]{0:T(512)S(1)}, f32[512]{0:T(512)}, u32[]{:S(2)}) copy-start(f32[512]{0:T(512)} %param.31) | copy-start | bytes 6148
  830.4 55.4 %copy-start.26 = (f32[1024]{0:T(1024)S(1)}, f32[1024]{0:T(1024)}, u32[]{:S(2)}) copy-start(f32[1024]{0:T(1024)} %copy-done.25) | copy-start | bytes 12292
  830.4 55.4 %copy-start.23 = (f32[1024]{0:T(1024)S(1)}, f32[1024]{0:T(1024)}, u32[]{:S(2)}) copy-start(f32[1024]{0:T(1024)} %copy-done.22) | copy-start | bytes 12292
  830.7 62.7 %copy-start.9 = (bf16[1,1024,512]{2,1,0:T(8,128)(2,1)S(1)}, bf16[1,1024,512]{2,1,0:T(8,128)(2,1)}, u32[]{:S(2)}) copy-start(bf16[1,1024,512]{2,1,0:T(8,128)(2,1)} %param.37) | copy-start | bytes 3145732
  831.4 57.5 %all-to-all-start = ((bf16[8,3,64,128]{3,2,1,0:T(8,128)(2,1)}), bf16[8,3,64,128]{3,2,1,0:T(8,128)(2,1)S(1)}, u32[]{:S(2)}, u32[]{:S(2)}) async-start(bf16[8,3,64,128]{3,2,1,0:T(8,128)(2,1)} %copy.79), calls=%async_computation.4 | async-start | bytes 786432 | tf_op jit(solution)/shard_map/all_to_all | solution.py:21
  889.0 21.2 %all-to-all-start.1 = ((bf16[8,64,1152]{2,1,0:T(8,128)(2,1)}), bf16[8,64,1152]{2,1,0:T(8,128)(2,1)}, u32[]{:S(2)}, u32[]{:S(2)}) async-start(bf16[8,64,1152]{2,1,0:T(8,128)(2,1)} %bitcast.206), calls=%async_computation.5 | async-start | bytes 2359296 | tf_op jit(solution)/shard_map/all_to_all | solution.py:21
  893.2 138.4 %all-reduce.3.cloned.1.call-start = ((), (), s32[]{:S(2)}) async-start(), calls=%async_computation.14 | async-start | bytes 2097152 | tf_op jit(solution)/shard_map/psum | solution.py:252
  893.3 5.0 copy-start.39
  893.3 140.6 %copy-start.1 = (f32[512,512]{1,0:T(8,128)S(1)}, f32[512,512]{1,0:T(8,128)}, u32[]{:S(2)}) copy-start(f32[512,512]{1,0:T(8,128)} %param.29) | copy-start | bytes 3145732
  897.7 15.3 %copy-start.29 = (f32[2048]{0:T(1024)S(1)}, f32[2048]{0:T(1024)}, u32[]{:S(2)}) copy-start(f32[2048]{0:T(1024)} %copy-done.28) | copy-start | bytes 24580
  897.7 15.3 %copy-start.37 = (f32[512]{0:T(512)S(1)}, f32[512]{0:T(512)}, u32[]{:S(2)}) copy-start(f32[512]{0:T(512)} %get-tuple-element.163) | copy-start | bytes 6148
  897.7 15.3 %copy-start.38 = (f32[512]{0:T(512)S(1)}, f32[512]{0:T(512)}, u32[]{:S(2)}) copy-start(f32[512]{0:T(512)} %get-tuple-element.160) | copy-start | bytes 6148
  897.7 15.3 %copy-start.40 = (f32[512]{0:T(512)S(1)}, f32[512]{0:T(512)}, u32[]{:S(2)}) copy-start(f32[512]{0:T(512)} %get-tuple-element.158) | copy-start | bytes 6148
  897.7 15.3 %copy-start.41 = (f32[512]{0:T(512)S(1)}, f32[512]{0:T(512)}, u32[]{:S(2)}) copy-start(f32[512]{0:T(512)} %get-tuple-element.162) | copy-start | bytes 6148
  897.7 15.3 %copy-start.42 = (f32[512]{0:T(512)S(1)}, f32[512]{0:T(512)}, u32[]{:S(2)}) copy-start(f32[512]{0:T(512)} %get-tuple-element.224) | copy-start | bytes 6148
  (11 other events, 20.6 us)
Sparse Core Ops, SparseCore 0:
  15.9 83.4 all-gather.4
  156.9 142.9 reduce-scatter.4
  303.9 81.5 all-gather.6
  386.9 79.2 all-gather.8
  483.1 75.2 reduce-scatter.8
  560.7 77.2 reduce-scatter.6
  644.0 81.2 all-gather.10
  807.8 75.2 reduce-scatter.10
  900.7 130.9 all-reduce.2
where the time goes:
time: 1040 us
  waiting for transfers between devices  700 us (67%)
  matrix products  127 us (12%)
  blocking collectives  81.5 us (8%)
  other arithmetic  71.6 us (7%)
  local copies, waits for them, and re-layouts  35.8 us (3%)
  between operations  15.5 us (1%)
    reduce_scatter x1, waiting for transfers between devices, shards(): lax.psum_scatter(jnp.einsum('nse,de->nsd', part_rows, out_copy, preferred...  143 us
    all_gather x1, waiting for transfers between devices, shards(): grad_attn_all = lax.all_gather(grad_attn, 'tensor', axis=0, tiled=True)  81.2 us
    psum x1, waiting for transfers between devices, shards(): lax.psum((grad_time_w, grad_time_bias, grad_gain_one, grad_bias_one, grad...  77.5 us
    reduce_scatter x1, waiting for transfers between devices, shards(): lax.psum_scatter(jnp.einsum('nsf,df->nsd', part_rows, down_copy, preferre...  76.8 us
    all_gather x1, waiting for transfers between devices, shards(): grad_out_all = lax.all_gather(cotangent, 'tensor', axis=0, tiled=True)  72.8 us
    reduce_scatter x1, waiting for transfers between devices, shards(): lax.psum_scatter(jnp.einsum('nsf,df->nsd', part_rows, up_copy, preferred_...  66.5 us
    all_gather x1, waiting for transfers between devices, shards(): normed_all = lax.all_gather(normed_one, 'tensor', axis=0, tiled=True)  63.1 us
    all_gather x1, waiting for transfers between devices, shards(): second_all = lax.all_gather(normed_two, 'tensor', axis=0, tiled=True)  60.2 us
  transfers between devices with their start and end apart: 11, of which 10 were waited for; matrix products, arithmetic and copies ran while one was open for 6% of the time, Pallas kernels for 0%

commit v1 on v0

--- a/solution.py
+++ b/solution.py
@@ -249,19 +249,18 @@
             1,
         ),
     )
-    summed = lax.psum(
-        (
-            grad_time_w,
-            grad_time_bias,
-            grad_gain_one,
-            grad_bias_one,
-            grad_gain_two,
-            grad_bias_two,
-            grad_bias_up,
-            grad_b_down,
-        ),
-        ("dp", "tensor"),
-    )
+    summed = (
+        grad_time_w,
+        grad_time_bias,
+        grad_gain_one,
+        grad_bias_one,
+        grad_gain_two,
+        grad_bias_two,
+        grad_bias_up,
+        grad_b_down,
+    )
+    for mesh_axis in ("tensor", "dp"):
+        summed = lax.psum(summed, mesh_axis)
     return (
         layer_out,
         grad_tokens,

time: 1040 us -> 1020 us (0.981)
  waiting for transfers between devices: 700 us -> 675 us
    psum x1 -> x2, waiting for transfers between devices: 77.5 us -> 61.9 us  [shards(): summed = lax.psum(summed, mesh_axis)]
    psum x1 -> x2, blocking collectives: 41.1 us -> 40.6 us  [shards(): summed = lax.psum(summed, mesh_axis)]
  transfers between devices with their start and end apart: 11 -> 12, of which waited for: 10 -> 10; matrix products, arithmetic and copies ran while one was open for 6% -> 6% of each run, Pallas kernels for 0% -> 0%
where the time goes in v1:
time: 1020 us
  waiting for transfers between devices  675 us (66%)
  matrix products  129 us (13%)
  blocking collectives  80.8 us (8%)
  other arithmetic  71.8 us (7%)
  local copies, waits for them, and re-layouts  35.2 us (3%)
  between operations  15.8 us (2%)
    reduce_scatter x1, waiting for transfers between devices, shards(): lax.psum_scatter(jnp.einsum('nse,de->nsd', part_rows, out_copy, preferred...  143 us
    all_gather x1, waiting for transfers between devices, shards(): grad_attn_all = lax.all_gather(grad_attn, 'tensor', axis=0, tiled=True)  80.9 us
    reduce_scatter x1, waiting for transfers between devices, shards(): lax.psum_scatter(jnp.einsum('nsf,df->nsd', part_rows, down_copy, preferre...  76.8 us
    all_gather x1, waiting for transfers between devices, shards(): grad_out_all = lax.all_gather(cotangent, 'tensor', axis=0, tiled=True)  72.8 us
    reduce_scatter x1, waiting for transfers between devices, shards(): lax.psum_scatter(jnp.einsum('nsf,df->nsd', part_rows, up_copy, preferred_...  66.6 us
    all_gather x1, waiting for transfers between devices, shards(): normed_all = lax.all_gather(normed_one, 'tensor', axis=0, tiled=True)  63.1 us
    psum x2, waiting for transfers between devices, shards(): summed = lax.psum(summed, mesh_axis)  61.9 us
    all_gather x1, waiting for transfers between devices, shards(): second_all = lax.all_gather(normed_two, 'tensor', axis=0, tiled=True)  60.4 us
  transfers between devices with their start and end apart: 12, of which 10 were waited for; matrix products, arithmetic and copies ran while one was open for 6% of the time, Pallas kernels for 0%

profile of v1, /device:TPU:0, one launch (start us, length us, event | category | flops | bytes accessed | tf_op | source)
XLA Modules:
  0.0 1016.9 jit_solution(5509889310444060920)
XLA Ops:
  13.0 2.7 add_convert_fusion.2
  15.9 10.7 %all_gather.26 = bf16[512,128]{1,0:T(8,128)(2,1)S(1)} all-gather(bf16[64,128]{1,0:T(8,128)(2,1)S(1)} %convert_element_type.133), channel_id=1, replica_groups=mesh['dp'=8,'tensor'=4] {'dp'}, dimensions={0}, use_global_device_ids=true | all-gather | bytes 147456 | tf_op jit(solution)/shard_map/all_gather | solution.py:140
  26.6 9.7 all_gather.25
  36.3 63.1 %all-gather.5.cloned.1.call-done = bf16[4,1024,512]{2,1,0:T(8,128)(2,1)} async-done(((bf16[1,1024,512]{2,1,0:T(8,128)(2,1)}), bf16[4,1024,512]{2,1,0:T(8,128)(2,1)}) %all-gather.5.cloned.1.call-update) | async-done | bytes 4194320 | tf_op jit(solution)/shard_map/all_gather | solution.py:152
  99.4 4.5 convert_bitcast_fusion
  109.8 42.4 %while.22 = (s32[]{:T(128)}, bf16[4,1024,128]{1,2,0:T(8,128)(2,1)S(1)}, f32[4,2,1024,1]{2,1,3,0:T(2,128)S(1)}, bf16[4,1024,128]{1,2,0:T(8,128)(2,1)S(1)}, s32[4,...) while((s32[]{:T(128)}, ...), condition=%wide.region_5.6_spmd, body=%wide.region_2.5_spmd.sunk | while | flops 566361088 | bytes 32585864 | solution.py:156
  117.5 2.8 fusion.136
  128.1 2.8 fusion.136
  138.7 2.8 fusion.136
  149.3 2.8 fusion.136
  152.2 4.5 fusion.69
  156.9 143.1 %reduce-scatter.5.cloned.1.call-done = f32[1,1024,512]{2,1,0:T(8,128)} async-done(((f32[4,1024,512]{2,1,0:T(8,128)}), f32[1,1024,512]{2,1,0:T(8,128)}) %reduce-scatter.5.cloned.1.call-update) | async-done | bytes 2097168 | tf_op jit(solution)/shard_map/reduce_scatter | solution.py:160
  305.2 10.0 all_gather.29
  315.2 9.8 all_gather.28
  325.0 60.4 %all-gather.7.cloned.1.call-done = bf16[4,1024,512]{2,1,0:T(8,128)(2,1)} async-done(((bf16[1,1024,512]{2,1,0:T(8,128)(2,1)}), bf16[4,1024,512]{2,1,0:T(8,128)(2,1)}) %all-gather.7.cloned.1.call-update) | async-done | bytes 4194320 | tf_op jit(solution)/shard_map/all_gather | solution.py:168
  385.4 8.0 fusion.64
  393.4 72.8 %all-gather.9.cloned.1.call-done = bf16[4,1024,512]{2,1,0:T(8,128)(2,1)} async-done(((bf16[1,1024,512]{2,1,0:T(8,128)(2,1)}), bf16[4,1024,512]{2,1,0:T(8,128)(2,1)}) %all-gather.9.cloned.1.call-update) | async-done | bytes 4194320 | tf_op jit(solution)/shard_map/all_gather | solution.py:185
  466.2 10.8 %convert_reduce_fusion = (f32[512]{0:T(512)}, bf16[4,1024,512]{2,1,0:T(8,128)(2,1)S(1)}) fusion(f32[4,1024,512]{2,1,0:T(8,128)} %fusion.64, f32[512]{0:T(512)S(1)} %dynamic_slice.43, bf16[4,1024,512]{2,1,0:T(8,128)(2,1)} %all-gather.9.cloned.1.call-done, bf16[512,512]{1,0:T(8,128)(2,1)S(1)} %all_gather.29), kind=kOutput, calls=%fused_computation.53 | convolution fusion | flops 2195717632 | bytes 17305600 | tf_op jit(solution)/shard_map/nsd,df->nsf/dot_general | solution.py:189
  479.0 4.5 convolution_convert_fusion
  483.6 8.8 convolution_convert_fusion.1
  492.4 66.6 %reduce-scatter.9.cloned.1.call-done = bf16[1,1024,512]{2,1,0:T(8,128)(2,1)} async-done(((bf16[4,1024,512]{2,1,0:T(8,128)(2,1)}), bf16[1,1024,512]{2,1,0:T(8,128)(2,1)}) %reduce-scatter.9.cloned.1.call-update) | async-done | bytes 1048592 | tf_op jit(solution)/shard_map/reduce_scatter | solution.py:197
  559.0 2.7 fusion.40
  561.7 76.8 %reduce-scatter.7.cloned.1.call-done = bf16[1,1024,512]{2,1,0:T(8,128)(2,1)} async-done(((bf16[4,1024,512]{2,1,0:T(8,128)(2,1)}), bf16[1,1024,512]{2,1,0:T(8,128)(2,1)}) %reduce-scatter.7.cloned.1.call-update) | async-done | bytes 1048592 | tf_op jit(solution)/shard_map/reduce_scatter | solution.py:175
  638.5 3.2 fusion.78
  644.9 80.9 %all-gather.11.cloned.1.call-done = bf16[4,1024,512]{2,1,0:T(8,128)(2,1)} async-done(((bf16[1,1024,512]{2,1,0:T(8,128)(2,1)}), bf16[4,1024,512]{2,1,0:T(8,128)(2,1)}) %all-gather.11.cloned.1.call-update) | async-done | bytes 4194320 | tf_op jit(solution)/shard_map/all_gather | solution.py:209
  725.9 3.4 convolution_convert_fusion.2
  729.3 72.7 %while.23 = (s32[]{:T(128)}, bf16[4,3,1024,128]{2,3,1,0:T(8,128)(2,1)}, bf16[4,1024,128]{1,2,0:T(8,128)(2,1)}, s32[4,1024]{1,0:T(4,128)S(1)}, s32[4]{0:T(128)S(1...) while((s32[]{:T(128)}, ...), condition=%wide.region_15.16_spmd, body=%wide.region_13.15_spmd.sunk | while | flops 1380842496 | bytes 73996440 | solution.py:214
  738.2 3.4 multiply_reduce_fusion.4
  741.6 2.7 multiply_convert_fusion.5
  756.3 3.4 multiply_reduce_fusion.4
  759.7 2.7 multiply_convert_fusion.5
  774.5 3.4 multiply_reduce_fusion.4
  792.6 3.4 multiply_reduce_fusion.4
  796.0 2.7 multiply_convert_fusion.5
  802.1 6.2 bitcast_convert_fusion
  809.0 6.8 fusion.47
  815.7 8.4 fusion.55
  826.9 3.7 all-to-all-start
  830.7 4.0 fusion.60
  834.8 49.1 %reduce-scatter.11.cloned.1.call-done = bf16[1,1024,512]{2,1,0:T(8,128)(2,1)} async-done(((bf16[4,1024,512]{2,1,0:T(8,128)(2,1)}), bf16[1,1024,512]{2,1,0:T(8,128)(2,1)}) %reduce-scatter.11.cloned.1.call-update) | async-done | bytes 1048592 | tf_op jit(solution)/shard_map/reduce_scatter | solution.py:222
  883.8 2.8 convert_reduce_fusion.1
  887.4 3.3 fusion.41
  890.7 3.6 fusion.77
  898.8 3.7 all-to-all-start.1
  902.8 45.7 %all-reduce.5.cloned.1.call-done = f32[512,512]{1,0:T(8,128)} async-done(((f32[512,512]{1,0:T(8,128)}), f32[512,512]{1,0:T(8,128)}) %all-reduce.5.cloned.1.call-update) | async-done | bytes 1048592 | tf_op jit(solution)/shard_map/psum | solution.py:263
  950.7 17.5 %all-reduce.1 = (f32[512]{0:T(512)S(1)}, f32[512]{0:T(512)S(1)}, f32[512]{0:T(512)S(1)}, f32[512]{0:T(512)S(1)}, f32[512]{0:T(512)S(1)}, /*index=5*/f32[2048]{0:T(1024)S(1)}, f32[512]{0:T(512)S(1)}) all-reduce(f32[512]{0:T(512)S(1)} %copy-done.28, f32[512]{0:T(512)S(1)} %copy-done.34, ...), channel_id=1, replica_groups=mesh['dp'=8,'tensor'=4] {'tensor'}, use_global_device_ids=true, to_apply=%region_24.25 | all-reduce | flops 5120 | bytes 40960 | tf_op jit(solution)/shard_map/psum | solution.py:263
  968.3 23.0 %all-reduce = (f32[512]{0:T(512)}, f32[512]{0:T(512)}, f32[512]{0:T(512)}, f32[512]{0:T(512)}, f32[512]{0:T(512)}, /*index=5*/f32[2048]{0:T(1024)}, f32[512]{0:T(512)}) all-reduce(f32[512]{0:T(512)S(1)} %get-tuple-element.206, f32[512]{0:T(512)S(1)} %get-tuple-element.207, ...), channel_id=1, replica_groups=mesh['dp'=8,'tensor'=4] {'dp'}, use_global_device_ids=true, to_apply=%region_25.26 | all-reduce | flops 5120 | bytes 40960 | tf_op jit(solution)/shard_map/psum | solution.py:263
  991.3 16.3 %all-reduce.7.cloned.1.call-done = f32[512,512]{1,0:T(8,128)} async-done(((f32[512,512]{1,0:T(8,128)}), f32[512,512]{1,0:T(8,128)}) %all-reduce.7.cloned.1.call-update) | async-done | bytes 1048592 | tf_op jit(solution)/shard_map/psum | solution.py:263
  (256 shorter events, 116.2 us)
Async XLA Ops:
  7.2 8.6 copy-start.25
  7.2 8.6 copy-start.21
  7.2 92.1 %all-gather.5.cloned.1.call-start = ((), (), s32[]{:S(2)}) async-start(), calls=%async_computation.6 | async-start | bytes 5242880 | tf_op jit(solution)/shard_map/all_gather | solution.py:152
  9.7 290.2 %copy-start.18 = (f32[512]{0:T(512)}, f32[512]{0:T(512)S(1)}, u32[]{:S(2)}) copy-start(f32[512]{0:T(512)S(1)} %add.154) | copy-start | bytes 6148
  11.3 4.6 copy-start.14
  15.7 284.2 %reduce-scatter.5.cloned.1.call-start = ((), (), s32[]{:S(2)}) async-start(), calls=%async_computation.7 | async-start | bytes 10485760 | tf_op jit(solution)/shard_map/reduce_scatter | solution.py:160
  36.3 67.6 %copy-start.12 = (bf16[3,512,128]{2,1,0:T(8,128)(2,1)}, bf16[3,512,128]{2,1,0:T(8,128)(2,1)S(1)}, u32[]{:S(2)}) copy-start(bf16[3,512,128]{2,1,0:T(8,128)(2,1)S(1)} %all_gather.25) | copy-start | bytes 1179652
  105.4 4.3 copy-start.20
  105.4 4.3 copy-start.45
  152.2 4.5 copy-start.6
  152.2 4.5 copy-start.7
  152.2 4.5 copy-start.11
  156.7 143.2 %copy-start.2 = (bf16[1,1024,512]{2,1,0:T(8,128)(2,1)S(1)}, bf16[1,1024,512]{2,1,0:T(8,128)(2,1)}, u32[]{:S(2)}) copy-start(bf16[1,1024,512]{2,1,0:T(8,128)(2,1)} %param.21) | copy-start | bytes 3145732
  156.8 145.5 %copy-start.26 = (f32[512]{0:T(512)S(1)}, f32[512]{0:T(512)}, u32[]{:S(2)}) copy-start(f32[512]{0:T(512)} %param.33) | copy-start | bytes 6148
  156.8 145.5 %copy-start.39 = (f32[512]{0:T(512)S(1)}, f32[512]{0:T(512)}, u32[]{:S(2)}) copy-start(f32[512]{0:T(512)} %param.34) | copy-start | bytes 6148
  156.8 228.6 %all-gather.7.cloned.1.call-start = ((), (), s32[]{:S(2)}) async-start(), calls=%async_computation.8 | async-start | bytes 5242880 | tf_op jit(solution)/shard_map/all_gather | solution.py:168
  303.7 162.5 %all-gather.9.cloned.1.call-start = ((), (), s32[]{:S(2)}) async-start(), calls=%async_computation.10 | async-start | bytes 5242880 | tf_op jit(solution)/shard_map/all_gather | solution.py:185
  304.3 254.7 %reduce-scatter.9.cloned.1.call-start = ((), (), s32[]{:S(2)}) async-start(), calls=%async_computation.11 | async-start | bytes 5242880 | tf_op jit(solution)/shard_map/reduce_scatter | solution.py:197
  483.5 155.0 %reduce-scatter.7.cloned.1.call-start = ((), (), s32[]{:S(2)}) async-start(), calls=%async_computation.9 | async-start | bytes 5242880 | tf_op jit(solution)/shard_map/reduce_scatter | solution.py:175
  492.4 146.2 %copy-start.40 = (f32[512]{0:T(512)S(1)}, f32[512]{0:T(512)}, u32[]{:S(2)}) copy-start(f32[512]{0:T(512)} %param.36) | copy-start | bytes 6148
  492.4 233.5 %all-gather.11.cloned.1.call-start = ((), (), s32[]{:S(2)}) async-start(), calls=%async_computation.12 | async-start | bytes 5242880 | tf_op jit(solution)/shard_map/all_gather | solution.py:209
  561.7 81.3 %copy-start.8 = (bf16[1,1024,512]{2,1,0:T(8,128)(2,1)S(1)}, bf16[1,1024,512]{2,1,0:T(8,128)(2,1)}, u32[]{:S(2)}) copy-start(bf16[1,1024,512]{2,1,0:T(8,128)(2,1)} %param.37) | copy-start | bytes 3145732
  644.5 239.4 %reduce-scatter.11.cloned.1.call-start = ((), (), s32[]{:S(2)}) async-start(), calls=%async_computation.13 | async-start | bytes 5242880 | tf_op jit(solution)/shard_map/reduce_scatter | solution.py:222
  729.3 72.8 %copy-start.13 = (bf16[3,512,128]{2,1,0:T(8,128)(2,1)S(1)}, bf16[3,512,128]{2,1,0:T(8,128)(2,1)}, u32[]{:S(2)}) copy-start(bf16[3,512,128]{2,1,0:T(8,128)(2,1)} %copy-done.12) | copy-start | bytes 1179652
  802.1 6.3 copy-start.30
  802.1 6.3 copy-start.32
  809.0 6.8 copy-start.43
  815.7 8.4 copy-start.42
  815.7 8.4 copy-start.44
  826.9 71.8 %all-to-all-start = ((bf16[8,3,64,128]{3,2,1,0:T(8,128)(2,1)}), bf16[8,3,64,128]{3,2,1,0:T(8,128)(2,1)S(1)}, u32[]{:S(2)}, u32[]{:S(2)}) async-start(bf16[8,3,64,128]{3,2,1,0:T(8,128)(2,1)} %copy.79), calls=%async_computation.4 | async-start | bytes 786432 | tf_op jit(solution)/shard_map/all_to_all | solution.py:21
  830.6 53.2 %copy-start.3 = (bf16[1,1024,512]{2,1,0:T(8,128)(2,1)S(1)}, bf16[1,1024,512]{2,1,0:T(8,128)(2,1)}, u32[]{:S(2)}) copy-start(bf16[1,1024,512]{2,1,0:T(8,128)(2,1)} %param.21) | copy-start | bytes 3145732
  830.6 53.2 %copy-start.15 = (f32[1024]{0:T(1024)S(1)}, f32[1024]{0:T(1024)}, u32[]{:S(2)}) copy-start(f32[1024]{0:T(1024)} %copy-done.14) | copy-start | bytes 12292
  830.6 53.2 %copy-start.19 = (f32[512]{0:T(512)S(1)}, f32[512]{0:T(512)}, u32[]{:S(2)}) copy-start(f32[512]{0:T(512)} %copy-done.18) | copy-start | bytes 6148
  830.7 56.7 %copy-start.23 = (f32[1024]{0:T(1024)S(1)}, f32[1024]{0:T(1024)}, u32[]{:S(2)}) copy-start(f32[1024]{0:T(1024)} %copy-done.22) | copy-start | bytes 12292
  830.7 60.0 %copy-start.5 = (f32[1,1024,512]{2,1,0:T(8,128)S(1)}, f32[1,1024,512]{2,1,0:T(8,128)}, u32[]{:S(2)}) copy-start(f32[1,1024,512]{2,1,0:T(8,128)} %copy-done.4) | copy-start | bytes 6291460
  830.7 117.8 %all-reduce.5.cloned.1.call-start = ((), (), s32[]{:S(2)}) async-start(), calls=%async_computation.14 | async-start | bytes 2097152 | tf_op jit(solution)/shard_map/psum | solution.py:263
  883.8 6.9 copy-start.9
  883.8 6.9 copy-start.10
  896.0 6.5 copy-start.41
  897.3 53.4 %copy-start.28 = (f32[512]{0:T(512)S(1)}, f32[512]{0:T(512)}, u32[]{:S(2)}) copy-start(f32[512]{0:T(512)} %copy-done.27) | copy-start | bytes 6148
  897.3 53.4 %copy-start.33 = (f32[512]{0:T(512)S(1)}, f32[512]{0:T(512)}, u32[]{:S(2)}) copy-start(f32[512]{0:T(512)} %get-tuple-element.163) | copy-start | bytes 6148
  897.3 53.4 %copy-start.34 = (f32[512]{0:T(512)S(1)}, f32[512]{0:T(512)}, u32[]{:S(2)}) copy-start(f32[512]{0:T(512)} %get-tuple-element.160) | copy-start | bytes 6148
  897.3 53.4 %copy-start.36 = (f32[512]{0:T(512)S(1)}, f32[512]{0:T(512)}, u32[]{:S(2)}) copy-start(f32[512]{0:T(512)} %get-tuple-element.158) | copy-start | bytes 6148
  897.3 53.4 %copy-start.37 = (f32[512]{0:T(512)S(1)}, f32[512]{0:T(512)}, u32[]{:S(2)}) copy-start(f32[512]{0:T(512)} %get-tuple-element.162) | copy-start | bytes 6148
  897.3 53.4 %copy-start.38 = (f32[512]{0:T(512)S(1)}, f32[512]{0:T(512)}, u32[]{:S(2)}) copy-start(f32[512]{0:T(512)} %get-tuple-element.231) | copy-start | bytes 6148
  897.4 112.5 %copy-start.1 = (f32[512,512]{1,0:T(8,128)S(1)}, f32[512,512]{1,0:T(8,128)}, u32[]{:S(2)}) copy-start(f32[512,512]{1,0:T(8,128)} %param.29) | copy-start | bytes 3145732
  898.8 50.4 %all-to-all-start.1 = ((bf16[8,64,1152]{2,1,0:T(8,128)(2,1)}), bf16[8,64,1152]{2,1,0:T(8,128)(2,1)S(1)}, u32[]{:S(2)}, u32[]{:S(2)}) async-start(bf16[8,64,1152]{2,1,0:T(8,128)(2,1)} %bitcast.46), calls=%async_computation.5 | async-start | bytes 2359296 | tf_op jit(solution)/shard_map/all_to_all | solution.py:21
  902.4 105.1 %all-reduce.7.cloned.1.call-start = ((), (), s32[]{:S(2)}) async-start(), calls=%async_computation.15 | async-start | bytes 2097152 | tf_op jit(solution)/shard_map/psum | solution.py:263
  (11 other events, 24.1 us)
Sparse Core Ops, SparseCore 0:
  15.9 83.4 all-gather.4
  156.9 142.9 reduce-scatter.4
  303.8 81.5 all-gather.6
  386.9 79.2 all-gather.8
  483.6 75.2 reduce-scatter.8
  561.2 77.2 reduce-scatter.6
  644.6 81.2 all-gather.10
  808.5 75.2 reduce-scatter.10
  896.1 52.3 all-reduce.4
  951.5 56.0 all-reduce.6
